TPU v7x, 32 devices: a whole 2x2x4 slice. The times are simulated.
32 devices in a mesh: groups: 2 (over x), frame: 8 (over z, y), band: 2 (over core).
Axes of the slice: x: 2, y: 2, z: 4, core: 2. Of those that a mesh axis runs over, the one named last changes fastest.
Arguments:
- hidden_in: bfloat16 [16, 1536, 1152], P(('groups', 'frame'), 'band'), parts along dimension 0, may hold values from -6 to 6
- latents: float32 [16, 192, 128], P(('groups', 'frame'), 'band'), parts along dimension 0, may hold values from -6 to 6
- fresh_noise: float32 [384, 128], P(('groups', 'band')), parts along dimension 0, may hold values from -6 to 6
- level_index: int32 [16], P(('groups', 'frame')), parts along dimension 0, may hold values from 1 to 31
- time_table: int32 [32], replicated, may hold values from 0 to 999, as said below
- frame_offset: int32 [2], P('groups'), parts along dimension 0, may hold values from 0 to 1023
- mod_table: float32 [3456], replicated, may hold values from -3 to 3
- time_weight: bfloat16 [128, 3456], replicated, may hold values from -0.5 to 0.5
- spatial_qkv: bfloat16 [1152, 1728], replicated, may hold values from -6 to 6
- spatial_out: bfloat16 [576, 1152], replicated, may hold values from -0.25 to 0.25
- temporal_qkv: bfloat16 [1152, 1728], replicated, may hold values from -6 to 6
- temporal_out: bfloat16 [576, 1152], replicated, may hold values from -0.25 to 0.25
- final_gain: float32 [1152], replicated, may hold values from 0.5 to 1.5
- out_weight: bfloat16 [1152, 16], replicated, may hold values from -0.1875 to 0.1875
Outputs:
- hidden_out: bfloat16 [16, 1536, 1152], P(('groups', 'frame'), 'band'), parts along dimension 0
- velocity: float32 [16, 192, 128], P(('groups', 'frame'), 'band'), parts along dimension 0
- next_latents: float32 [16, 192, 128], P(('groups', 'frame'), 'band'), parts along dimension 0
There are 2 independent parts, one for each index of `groups`. A program takes and returns all parts, laid end to end along the dimension named above; an argument that names none is the same for every part. Nothing has to cross between parts.
Inputs may be any that keep to these rules, and one draw needn't show every extreme that they name: `time_table`: entries rise strictly along the table, from 0 at the first entry to 999 at the last.
All inputs are finite; a program needn't handle non-finite values.
Results may differ from a plain program's by a relative error of at most 0.025.
Values may be sent and summed in bfloat16 or wider, within the bound.
A program may use at most 128 MiB of HBM per device.

v0:
```python
import math

import jax
import jax.numpy as jnp
from jax import lax
from jax.sharding import PartitionSpec as P

HEAD_SIZE = 72


epsilon = 1e-06


def from_behind(value, axis, steps):
    count = lax.axis_size(axis)
    initial, last = (max(0, -steps), min(count, count - steps))
    return lax.ppermute(value, axis, [(source, source + steps) for source in range(initial, last)])


def layer_norm(values):
    average = jnp.mean(values, axis=-1, keepdims=True)
    centred = values - average
    variance = jnp.mean(centred * centred, axis=-1, keepdims=True)
    return centred * lax.rsqrt(variance + epsilon)


def sinusoid(position, feature_count, first_sine):
    half_width = feature_count // 2
    frequency = jnp.exp(-math.log(10000.0) * jnp.arange(half_width, dtype=jnp.float32) / half_width)
    angles = position.astype(jnp.float32)[:, None] * frequency[None, :]
    if first_sine:
        return jnp.concatenate([jnp.sin(angles), jnp.cos(angles)], axis=-1)
    return jnp.concatenate([jnp.cos(angles), jnp.sin(angles)], axis=-1)


def mix_frames(rows, head_count):
    frame_count = rows.shape[0]
    item_count = rows.shape[1]
    parted = rows.reshape(frame_count, item_count, 3, head_count, HEAD_SIZE)
    attention_scores = jnp.einsum(
        "fnhd,gnhd->nhfg", parted[:, :, 0], parted[:, :, 1], preferred_element_type=jnp.float32
    ) / math.sqrt(HEAD_SIZE)
    row_max = jnp.max(attention_scores, axis=-1, keepdims=True)
    attention_weight = jnp.exp(attention_scores - row_max).astype(jnp.bfloat16)
    denominator = jnp.sum(attention_weight, axis=-1, dtype=jnp.float32)
    weighted_sum = jnp.einsum(
        "nhfg,gnhd->fnhd", attention_weight, parted[:, :, 2], preferred_element_type=jnp.float32
    )
    mixed = weighted_sum / jnp.transpose(denominator, (2, 0, 1))[..., None]
    return mixed.astype(jnp.bfloat16).reshape(frame_count, item_count, head_count * HEAD_SIZE)


def body(
    hidden_in,
    latents,
    fresh_noise,
    level_index,
    time_table,
    frame_offset,
    mod_table,
    time_weight,
    spatial_qkv,
    spatial_out,
    temporal_qkv,
    temporal_out,
    final_gain,
    out_weight,
):
    tokens = hidden_in.shape[1]
    model_width = hidden_in.shape[2]
    attended = spatial_out.shape[0]
    head_count = attended // HEAD_SIZE
    peers = lax.axis_size("frame")
    table_index = jnp.arange(time_table.shape[0], dtype=jnp.int32)
    now_steps = jnp.sum(
        jnp.where(table_index[None, :] == level_index[:, None], time_table[None, :], 0), axis=1
    )
    next_steps = jnp.sum(
        jnp.where(table_index[None, :] == level_index[:, None] - 1, time_table[None, :], 0), axis=1
    )
    activated = jax.nn.silu(sinusoid(now_steps, time_weight.shape[0], False)).astype(jnp.bfloat16)
    modulation = mod_table[None, :] + jnp.dot(
        activated, time_weight, preferred_element_type=jnp.float32
    )
    shift_part = modulation[:, :model_width]
    scale_part = modulation[:, model_width : 2 * model_width]
    gate_part = modulation[:, 2 * model_width :]
    inputs = hidden_in[0].astype(jnp.float32)
    normed = (layer_norm(inputs) * (1.0 + scale_part) + shift_part).astype(jnp.bfloat16)
    projected = jnp.dot(normed, spatial_qkv, preferred_element_type=jnp.float32).astype(
        jnp.bfloat16
    )
    query_rows = projected[:, :attended].reshape(tokens, head_count, HEAD_SIZE)
    key_value = projected[:, attended:]
    block_rows = lax.all_gather(key_value, "band", axis=0, tiled=True)
    row_max = jnp.full((head_count, tokens), -1e30, jnp.float32)
    row_count = block_rows.shape[0]
    key_matrix_rows = block_rows[:, :attended].reshape(row_count, head_count, HEAD_SIZE)
    value_matrix_rows = block_rows[:, attended:].reshape(row_count, head_count, HEAD_SIZE)
    attention_scores = jnp.einsum(
        "ubg,wbg->buw", query_rows, key_matrix_rows, preferred_element_type=jnp.float32
    ) / math.sqrt(HEAD_SIZE)
    new_max = jnp.maximum(row_max, jnp.max(attention_scores, axis=-1))
    attention_weight = jnp.exp(attention_scores - new_max[:, :, None]).astype(jnp.bfloat16)
    denominator = jnp.sum(attention_weight, axis=-1, dtype=jnp.float32)
    weighted_sum = jnp.einsum(
        "leq,qlr->ler", attention_weight, value_matrix_rows, preferred_element_type=jnp.float32
    )
    row_max, denominator, weighted_sum = (new_max, denominator, weighted_sum)
    spatial_mixed = (
        jnp.transpose(weighted_sum / denominator[:, :, None], (1, 0, 2))
        .reshape(tokens, attended)
        .astype(jnp.bfloat16)
    )
    residual = inputs + gate_part * jnp.dot(
        spatial_mixed, spatial_out, preferred_element_type=jnp.float32
    )
    position = lax.axis_index("frame") + frame_offset
    placed = sinusoid(position, model_width, True)
    temporal_in = (residual + placed).astype(jnp.bfloat16)
    spread_rows = temporal_in.reshape(1, peers, tokens // peers, model_width)
    gathered = lax.all_to_all(spread_rows, "frame", split_axis=1, concat_axis=0, tiled=True)
    frame_count = gathered.shape[0]
    item_count = gathered.shape[2]
    rows = jnp.dot(
        gathered.reshape(frame_count * item_count, model_width),
        temporal_qkv,
        preferred_element_type=jnp.float32,
    ).astype(jnp.bfloat16)
    mixed = mix_frames(rows.reshape(frame_count, item_count, 3 * attended), head_count)
    mixed_rows = mixed.reshape(frame_count, 1, item_count, attended)
    mixed_pairs = mixed_rows.reshape(mixed_rows.shape[0], 1, mixed_rows.shape[2] // 2, 2 * attended)
    returned = lax.all_to_all(mixed_pairs, "frame", split_axis=0, concat_axis=1, tiled=True)
    temporal_mixed = returned.reshape(tokens, attended)
    residual = residual + gate_part * jnp.dot(
        temporal_mixed, temporal_out, preferred_element_type=jnp.float32
    )
    hidden_out = residual.astype(jnp.bfloat16)[None]
    final_rows = (layer_norm(residual) * final_gain).astype(jnp.bfloat16)
    velocity = jnp.dot(final_rows, out_weight, preferred_element_type=jnp.float32).reshape(
        1, latents.shape[1], 128
    )
    time_delta = (next_steps - now_steps).astype(jnp.float32) / 1000.0
    update = latents + time_delta[:, None, None] * velocity
    shifted = from_behind(update.astype(jnp.bfloat16), "frame", 1).astype(update.dtype)
    next_latents = jnp.where(lax.axis_index("frame") == 0, fresh_noise[None], shifted)
    return (hidden_out, velocity, next_latents)


def solution(mesh):
    placed = (
        P(("groups", "frame"), "band", None),
        P(("groups", "frame"), "band", None),
        P(("groups", "band"), None),
        P(("groups", "frame")),
        P(),
        P("groups"),
        P(),
        P(),
        P(),
        P(),
        P(),
        P(),
        P(),
        P(),
    )
    return jax.shard_map(
        body,
        mesh=mesh,
        in_specs=placed,
        out_specs=(
            P(("groups", "frame"), "band", None),
            P(("groups", "frame"), "band", None),
            P(("groups", "frame"), "band", None),
        ),
        check_vma=False,
    )
```

profile of v0, /device:TPU:0, one launch (start us, length us, event | category | flops | bytes accessed | tf_op | source)
XLA Modules:
  0.0 232.9 jit_solution(8526192935074219680)
XLA Ops:
  14.9 5.9 %convolution_convert_fusion.1 = bf16[768,1728]{0,1:T(8,128)(2,1)S(1)} fusion(bf16[1152,1728]{0,1:T(8,128)(2,1)} %param.22, bf16[1,768,1152]{2,1,0:T(8,128)(2,1)S(1)} %copy-done.1, f32[1152]{0:T(1024)S(1)} %get-tuple-element.4, f32[1152]{0:T(1024)S(1)} %get-tuple-element.5, f32[768]{0:T(1024)S(1)} %add_rsqrt_fusion.1, f32[768]{0:T(1024)S(1)} %broadcast_multiply_fusion.1), kind=kOutput, calls=%fused_computation.21 | convolution fusion | flops 3064283136 | bytes 8420352 | tf_op jit(solution)/shard_map/dot_general | solution.py:90
  24.5 14.7 %all-gather.2.cloned.1.call-done = bf16[1536,1152]{0,1:T(8,128)(2,1)} async-done(((bf16[768,1152]{0,1:T(8,128)(2,1)}), bf16[1536,1152]{0,1:T(8,128)(2,1)}) %all-gather.2.cloned.1.call-update) | async-done | bytes 3538960 | tf_op jit(solution)/shard_map/all_gather | solution.py:95
  39.3 3.5 %fusion.45 = (bf16[1536,576]{0,1:T(8,128)(2,1)S(1)}, bf16[1536,576]{0,1:T(8,128)(2,1)}) fusion(bf16[1536,1152]{0,1:T(8,128)(2,1)} %all-gather.2.cloned.1.call-done), kind=kLoop, calls=%fused_computation.79 | loop fusion | bytes 7077888 | tf_op jit(solution)/shard_map/slice | solution.py:98
  42.8 14.8 %multiply_reduce_fusion = (f32[8,768]{1,0:T(8,128)S(1)}, f32[8,768,1536]{2,1,0:T(8,128)}) fusion(bf16[768,8,72]{0,2,1:T(8,128)(2,1)S(1)} %bitcast.79, bf16[1536,8,72]{0,2,1:T(8,128)(2,1)S(1)} %bitcast.78), kind=kOutput, calls=%fused_computation.3 | convolution fusion | flops 1377822720 | bytes 40427520 | tf_op jit(solution)/shard_map/ubg,wbg->buw/dot_general | solution.py:100
  57.6 16.7 %convert_reduce_fusion = f32[8,768]{1,0:T(8,128)S(1)} fusion(f32[8,768]{1,0:T(8,128)S(1)} %broadcast_maximum_fusion, f32[8,768,1536]{2,1,0:T(8,128)} %get-tuple-element.16), kind=kLoop, calls=%fused_computation.1 | loop fusion | flops 47179776 | bytes 37797888 | tf_op jit(solution)/shard_map/reduce_sum | solution.py:105
  74.3 16.7 %fusion.13 = bf16[768,8,72]{0,2,1:T(8,128)(2,1)} fusion(bf16[1536,8,72]{0,2,1:T(8,128)(2,1)} %bitcast.81, f32[8,768,1536]{2,1,0:T(8,128)} %get-tuple-element.16, f32[8,768]{1,0:T(8,128)S(1)} %broadcast_maximum_fusion, f32[768,8]{0,1:T(8,128)S(1)} %bitcast.85), kind=kOutput, calls=%fused_computation.26 | convolution fusion | flops 1388150784 | bytes 40452096 | tf_op jit(solution)/shard_map/leq,qlr->ler/dot_general | solution.py:106
  91.0 5.0 %add_convert_fusion = (bf16[768,1152]{1,0:T(8,128)(2,1)S(1)}, f32[768,1152]{1,0:T(8,128)}) fusion(f32[1152]{0:T(1024)S(1)} %maximum_reduce_fusion, bf16[768,576]{0,1:T(8,128)(2,1)} %bitcast.86, bf16[576,1152]{1,0:T(8,128)(2,1)S(1)} %copy-done, f32[1152]{0:T(1024)S(1)} %get-tuple-element.3, bf16[1,768,1152]{2,1,0:T(8,128)(2,1)S(1)} %copy-done.1), kind=kOutput, calls=%fused_computation.19 | convolution fusion | flops 1023639552 | bytes 9298944 | tf_op jit(solution)/shard_map/dot_general | solution.py:115
  95.9 47.3 %all_to_all.8 = bf16[1,8,96,1152]{3,2,0,1:T(8,128)(2,1)S(1)} all-to-all(bf16[1,8,96,1152]{3,2,0,1:T(8,128)(2,1)S(1)} %bitcast.82), channel_id=1, replica_groups=mesh['groups'=2,'frame'=8,'band'=2] {'frame'}, dimensions={1} | all-to-all | bytes 3538944 | tf_op jit(solution)/shard_map/all_to_all | solution.py:122
  143.2 5.0 %convolution_convert_fusion = bf16[768,1728]{0,1:T(8,128)(2,1)} fusion(bf16[768,1152]{1,0:T(8,128)(2,1)S(1)} %bitcast.83, bf16[1152,1728]{0,1:T(8,128)(2,1)S(1)} %copy-done.9), kind=kOutput, calls=%fused_computation.20 | convolution fusion | flops 3058974720 | bytes 8404992 | tf_op jit(solution)/shard_map/dot_general | solution.py:125
  148.2 7.0 %reshape_reshape.3 = bf16[8,96,3,8,72]{1,0,4,3,2:T(8,128)(2,1)} reshape(bf16[768,1728]{0,1:T(8,128)(2,1)} %convolution_convert_fusion) | data formatting | bytes 5308416 | tf_op jit(solution)/shard_map/reshape;reshape | solution.py:39
  155.2 4.0 %fusion.44 = (bf16[8,96,1,8,72]{1,0,4,3,2:T(8,128)(2,1)}, bf16[8,96,1,8,72]{1,0,4,3,2:T(8,128)(2,1)}, bf16[8,96,1,8,72]{1,0,4,3,2:T(8,128)(2,1)}) fusion(bf16[8,96,3,8,72]{1,0,4,3,2:T(8,128)(2,1)} %reshape_reshape.3), kind=kLoop, calls=%fused_computation.78 | loop fusion | bytes 5308416 | tf_op jit(solution)/shard_map/slice | solution.py:47
  159.2 3.9 %copy.56 = bf16[8,96,1,8,72]{4,0,3,1,2:T(8,128)(2,1)S(1)} copy(bf16[8,96,1,8,72]{1,0,4,3,2:T(8,128)(2,1)} %get-tuple-element.11) | data formatting | bytes 1769472
  163.1 4.6 %copy.57 = bf16[8,96,1,8,72]{4,0,3,1,2:T(8,128)(2,1)} copy(bf16[8,96,1,8,72]{1,0,4,3,2:T(8,128)(2,1)} %get-tuple-element.12) | data formatting | bytes 1769472
  167.6 4.0 %fusion.19 = f32[96,8,8,8]{2,3,1,0:T(8,128)} fusion(bf16[8,96,1,8,72]{4,0,3,1,2:T(8,128)(2,1)} %copy.57, bf16[8,96,1,8,72]{4,0,3,1,2:T(8,128)(2,1)S(1)} %copy.56), kind=kOutput, calls=%fused_computation.33 | convolution fusion | flops 7077888 | bytes 1966080 | tf_op jit(solution)/shard_map/fnhd,gnhd->nhfg/dot_general | solution.py:40
  171.7 3.2 %copy.48 = f32[96,8,8,8]{0,3,2,1:T(8,128)S(1)} copy(f32[96,8,8,8]{2,3,1,0:T(8,128)} %fusion.19) | data formatting | bytes 393216 | tf_op jit(solution)/shard_map/fnhd,gnhd->nhfg/dot_general | solution.py:40
  175.0 2.9 %copy.49 = bf16[96,8,8,8]{3,2,1,0:T(8,128)(2,1)} copy(bf16[96,8,8,8]{0,3,2,1:T(8,128)(2,1)S(1)} %get-tuple-element.20) | data formatting | bytes 196608 | tf_op jit(solution)/shard_map/convert_element_type | solution.py:44
  178.2 3.4 %copy.55 = bf16[8,96,1,8,72]{4,0,3,1,2:T(8,128)(2,1)} copy(bf16[8,96,1,8,72]{1,0,4,3,2:T(8,128)(2,1)S(1)} %copy-done.3) | data formatting | bytes 1769472
  181.6 3.0 %fusion.10 = bf16[8,96,8,72]{3,0,2,1:T(8,128)(2,1)S(1)} fusion(bf16[96,8,8,8]{3,2,1,0:T(8,128)(2,1)} %copy.49, bf16[8,96,1,8,72]{4,0,3,1,2:T(8,128)(2,1)} %copy.55, f32[8,96,8]{0,2,1:T(8,128)S(1)} %copy.50), kind=kOutput, calls=%fused_computation.23 | convolution fusion | flops 7962624 | bytes 1892352 | tf_op jit(solution)/shard_map/nhfg,gnhd->fnhd/dot_general | solution.py:46
  184.8 2.5 %reshape_reshape_reshape.3 = bf16[8,1,48,1152]{3,2,0,1:T(8,128)(2,1)} reshape(bf16[8,96,8,72]{3,2,1,0:T(8,128)(2,1)S(1)} %copy.51) | data formatting | bytes 1769472 | tf_op jit(solution)/shard_map/reshape;reshape;reshape | solution.py:132
  187.3 3.8 %all-to-all-start.1 = ((bf16[8,1,48,1152]{3,2,1,0:T(8,128)(2,1)}), bf16[8,1,48,1152]{3,2,1,0:T(8,128)(2,1)S(1)}, u32[]{:S(2)}, u32[]{:S(2)}) async-start(bf16[8,1,48,1152]{3,2,1,0:T(8,128)(2,1)} %bitcast.80), calls=%async_computation.1 | async-start | bytes 1769472 | tf_op jit(solution)/shard_map/all_to_all | solution.py:133
  192.4 20.9 %all-to-all-done.1 = bf16[8,1,48,1152]{3,2,1,0:T(8,128)(2,1)S(1)} async-done(((bf16[8,1,48,1152]{3,2,1,0:T(8,128)(2,1)}), bf16[8,1,48,1152]{3,2,1,0:T(8,128)(2,1)S(1)}, u32[]{:S(2)}, u32[]{:S(2)}) %all-to-all-start.1) | async-done | bytes 884768 | tf_op jit(solution)/shard_map/all_to_all | solution.py:133
  213.9 4.1 %fusion.46 = (f32[768]{0:T(1024)S(1)}, f32[768,1152]{1,0:T(8,128)S(1)}) fusion(f32[768,1152]{1,0:T(8,128)} %get-tuple-element.18, bf16[768,576]{1,0:T(8,128)(2,1)S(1)} %reshape.171, bf16[576,1152]{1,0:T(8,128)(2,1)} %param.25, f32[1152]{0:T(1024)S(1)} %get-tuple-element.3), kind=kOutput, calls=%fused_computation.80 | convolution fusion | flops 1021869312 | bytes 9297408 | tf_op jit(solution)/shard_map/dot_general | solution.py:135
  218.1 1.8 multiply_reduce_fusion.1
  220.8 3.1 %collective-permute-start = (bf16[1,96,128]{2,1,0:T(8,128)(2,1)S(1)}, bf16[1,96,128]{2,1,0:T(8,128)(2,1)S(1)}, u32[]{:S(2)}, u32[]{:S(2)}) collective-permute-start(bf16[1,96,128]{2,1,0:T(8,128)(2,1)S(1)} %add_convert_fusion.1), channel_id=1, source_target_pairs={{0,2},{2,4},{4,6},{6,8},{8,10},{10,12},{12,14},{1,3},{3,5},{5,7},{... | collective-permute-start | bytes 73736 | tf_op jit(solution)/shard_map/ppermute | solution.py:17
  (49 shorter events, 13.4 us)
Async XLA Ops:
  7.2 83.8 %copy-start = (bf16[576,1152]{1,0:T(8,128)(2,1)S(1)}, bf16[576,1152]{1,0:T(8,128)(2,1)}, u32[]{:S(2)}) copy-start(bf16[576,1152]{1,0:T(8,128)(2,1)} %param.23) | copy-start | bytes 3981316
  7.2 7.1 %copy-start.1 = (bf16[1,768,1152]{2,1,0:T(8,128)(2,1)S(1)}, bf16[1,768,1152]{2,1,0:T(8,128)(2,1)}, u32[]{:S(2)}) copy-start(bf16[1,768,1152]{2,1,0:T(8,128)(2,1)} %param.14) | copy-start | bytes 5308420
  7.2 32.1 %all-gather.2.cloned.1.call-start = ((), (), s32[]{:S(2)}) async-start(), calls=%async_computation.2 | async-start | bytes 5308416 | tf_op jit(solution)/shard_map/all_gather | solution.py:95
  20.8 1.5 copy-start.2
  39.3 3.5 %slice-start = ((bf16[768,1728]{0,1:T(8,128)(2,1)}), bf16[768,576]{0,1:T(8,128)(2,1)S(1)}, s32[]{:S(2)}) async-start(bf16[768,1728]{0,1:T(8,128)(2,1)} %copy-done.2), calls=%async_computation.3 | async-start | bytes 1769472 | tf_op jit(solution)/shard_map/slice | solution.py:93
  91.0 52.3 %copy-start.9 = (bf16[1152,1728]{0,1:T(8,128)(2,1)S(1)}, bf16[1152,1728]{0,1:T(8,128)(2,1)}, u32[]{:S(2)}) copy-start(bf16[1152,1728]{0,1:T(8,128)(2,1)} %param.24) | copy-start | bytes 11943940
  171.6 6.5 %copy-start.3 = (bf16[8,96,1,8,72]{1,0,4,3,2:T(8,128)(2,1)S(1)}, bf16[8,96,1,8,72]{1,0,4,3,2:T(8,128)(2,1)}, u32[]{:S(2)}) copy-start(bf16[8,96,1,8,72]{1,0,4,3,2:T(8,128)(2,1)} %get-tuple-element.10) | copy-start | bytes 2654212
  187.3 26.0 %all-to-all-start.1 = ((bf16[8,1,48,1152]{3,2,1,0:T(8,128)(2,1)}), bf16[8,1,48,1152]{3,2,1,0:T(8,128)(2,1)S(1)}, u32[]{:S(2)}, u32[]{:S(2)}) async-start(bf16[8,1,48,1152]{3,2,1,0:T(8,128)(2,1)} %bitcast.80), calls=%async_computation.1 | async-start | bytes 1769472 | tf_op jit(solution)/shard_map/all_to_all | solution.py:133
  218.0 1.9 copy-start.7
  218.0 1.9 copy-start.8
  219.9 0.9 copy-start.5
  219.9 5.6 %copy-start.6 = (f32[96,128]{1,0:T(8,128)S(1)}, f32[96,128]{1,0:T(8,128)}, u32[]{:S(2)}) copy-start(f32[96,128]{1,0:T(8,128)} %param.16) | copy-start | bytes 147460
  220.8 5.3 %copy-start.4 = (f32[1,96,128]{2,1,0:T(8,128)}, f32[1,96,128]{2,1,0:T(8,128)S(1)}, u32[]{:S(2)}) copy-start(f32[1,96,128]{2,1,0:T(8,128)S(1)} %reshape.172) | copy-start | bytes 147460
  220.8 4.6 %collective-permute-start = (bf16[1,96,128]{2,1,0:T(8,128)(2,1)S(1)}, bf16[1,96,128]{2,1,0:T(8,128)(2,1)S(1)}, u32[]{:S(2)}, u32[]{:S(2)}) collective-permute-start(bf16[1,96,128]{2,1,0:T(8,128)(2,1)S(1)} %add_convert_fusion.1), channel_id=1, source_target_pairs={{0,2},{2,4},{4,6},{6,8},{8,10},{10,12},{12,14},{1,3},{3,5},{5,7},{... | collective-permute-start | bytes 73736 | tf_op jit(solution)/shard_map/ppermute | solution.py:17
Sparse Core Ops, SparseCore 0:
  23.8 15.4 all-gather.1
where the time goes:
time: 234 us; the launch traced here: 233 us
  matrix products  60.7 us (26%)
  blocking collectives  47.3 us (20%)
  local copies, waits for them, and re-layouts  38.9 us (17%)
  waiting for transfers between devices  37.1 us (16%)
  other arithmetic  24.2 us (10%)
  between operations  17.7 us (8%)
  starting transfers between devices  6.96 us (3%)
    all_to_all x1, blocking collectives, body(): lax.all_to_all(spread_rows, 'frame', split_axis=1, concat_axis=0, tiled=T...  47.3 us
    all_to_all x1, waiting for transfers between devices, body(): lax.all_to_all(mixed_pairs, 'frame', split_axis=0, concat_axis=1, tiled=T...  20.9 us
    reduce_sum x1, other arithmetic, body(): denominator = jnp.sum(attention_weight, axis=-1, dtype=jnp.float32)  16.7 us
    dot_general x1, matrix products, body(): jnp.einsum('leq,qlr->ler', attention_weight, value_matrix_rows, preferred...  16.7 us
    dot_general x1, matrix products, body(): jnp.einsum('ubg,wbg->buw', query_rows, key_matrix_rows, preferred_element...  14.8 us
    all_gather x1, waiting for transfers between devices, body(): block_rows = lax.all_gather(key_value, 'band', axis=0, tiled=True)  14.7 us
    unnamed x23, local copies, waits for them, and re-layouts  13.4 us
    another operation x1, local copies, waits for them, and re-layouts, mix_frames(): parted = rows.reshape(frame_count, item_count, 3, head_count, HEAD_SIZE)  6.97 us
  transfers between devices with their start and end apart: 3, of which 3 were waited for; matrix products, arithmetic and copies ran while one was open for 0% of the time, Pallas kernels for 0%

commit v1 on v0

--- a/solution.py
+++ b/solution.py
@@ -1,8 +1,11 @@
+import functools
 import math
 
 import jax
 import jax.numpy as jnp
 from jax import lax
+from jax.experimental import pallas as pl
+from jax.experimental.pallas import tpu as pltpu
 from jax.sharding import PartitionSpec as P
 
 HEAD_SIZE = 72
@@ -50,7 +53,7 @@
     return mixed.astype(jnp.bfloat16).reshape(frame_count, item_count, head_count * HEAD_SIZE)
 
 
-def body(
+def plain_body(
     hidden_in,
     latents,
     fresh_noise,
@@ -147,6 +150,485 @@
     return (hidden_out, velocity, next_latents)
 
 
+MESH = pl.DeviceIdType.MESH
+ROWS = 256
+PAIR = 2
+GROUP = 16
+LANES = 128
+
+
+def block_kernel(
+    peers,
+    head_count,
+    hidden,
+    mod,
+    placed,
+    gain,
+    wide_weight,
+    time_delta,
+    latents,
+    noise,
+    spatial_qkv_hbm,
+    spatial_out_hbm,
+    temporal_qkv_hbm,
+    temporal_out_hbm,
+    hidden_out,
+    velocity_out,
+    next_out,
+    spatial_qkv,
+    spatial_out,
+    temporal_qkv,
+    temporal_out,
+    normed,
+    projected,
+    remote_kv,
+    query,
+    key,
+    value,
+    head_out,
+    mixed,
+    residual,
+    outgoing,
+    gathered,
+    temporal,
+    answer,
+    returned,
+    update_sent,
+    update_received,
+    weight_sem,
+    kv_send,
+    kv_recv,
+    fwd_send,
+    fwd_recv,
+    ret_send,
+    ret_recv,
+    next_send,
+    next_recv,
+):
+    f32, bf16 = jnp.float32, jnp.bfloat16
+    tokens, width = hidden.shape
+    attended = head_count * HEAD_SIZE
+    item = tokens // peers
+    me = lax.axis_index("frame")
+    mate = 1 - lax.axis_index("band")
+    pairs = peers // PAIR
+    my_pair = me // PAIR
+    chunk = PAIR * item
+    first_kv = attended // LANES * LANES
+    kv_shift = attended - first_kv
+    query_factor = math.log2(math.e) / math.sqrt(HEAD_SIZE)
+
+    loads = [
+        pltpu.make_async_copy(source, target, weight_sem.at[index])
+        for index, (source, target) in enumerate(
+            (
+                (spatial_qkv_hbm, spatial_qkv),
+                (spatial_out_hbm, spatial_out),
+                (temporal_qkv_hbm, temporal_qkv),
+                (temporal_out_hbm, temporal_out),
+            )
+        )
+    ]
+    for load in loads:
+        load.start()
+
+    barrier = pltpu.get_barrier_semaphore()
+    pl.semaphore_signal(barrier, inc=1, device_id={"band": mate}, device_id_type=MESH)
+    for step in range(1, peers):
+        pl.semaphore_signal(
+            barrier, inc=1, device_id={"frame": lax.rem(me + step, peers)}, device_id_type=MESH
+        )
+
+    column = lax.broadcasted_iota(jnp.int32, (1, 3 * attended), 1)
+    column_factor = jnp.where(column < attended, query_factor, 1.0).astype(f32)
+    gate = mod[:, 2 * width :]
+
+    def norm_step(index, carry):
+        rows = pl.ds(pl.multiple_of(index * 64, 64), 64)
+        lines = layer_norm(hidden[rows, :].astype(f32))
+        normed[rows, :] = (lines * (1.0 + mod[:, width : 2 * width]) + mod[:, :width]).astype(bf16)
+        return carry
+
+    lax.fori_loop(0, tokens // 64, norm_step, 0)
+    query[...] = jnp.zeros_like(query)
+    key[...] = jnp.zeros_like(key)
+    value[...] = jnp.ones_like(value)
+    pl.semaphore_wait(barrier, peers)
+    loads[0].wait()
+
+    def kv_copy(index):
+        rows = pl.ds(pl.multiple_of(index * ROWS, ROWS), ROWS)
+        return pltpu.make_async_remote_copy(
+            src_ref=projected.at[rows, pl.ds(first_kv, 3 * attended - first_kv)],
+            dst_ref=remote_kv.at[rows, :],
+            send_sem=kv_send.at[index],
+            recv_sem=kv_recv.at[index],
+            device_id={"band": mate},
+            device_id_type=MESH,
+        )
+
+    def project_step(index, carry):
+        rows = pl.ds(pl.multiple_of(index * ROWS, ROWS), ROWS)
+        product = jnp.dot(normed[rows, :], spatial_qkv[...], preferred_element_type=f32)
+        projected[rows, :] = (product * column_factor).astype(bf16)
+        kv_copy(index).start()
+        return carry
+
+    lax.fori_loop(0, tokens // ROWS, project_step, 0)
+
+    def split_own(index, carry):
+        rows = pl.ds(pl.multiple_of(index * ROWS, ROWS), ROWS)
+        for head in range(head_count):
+            low = head * HEAD_SIZE
+            query[head, rows, :HEAD_SIZE] = projected[rows, low : low + HEAD_SIZE]
+            low += attended
+            key[head, rows, :HEAD_SIZE] = projected[rows, low : low + HEAD_SIZE]
+            low += attended
+            value[head, rows, :HEAD_SIZE] = projected[rows, low : low + HEAD_SIZE]
+        return carry
+
+    lax.fori_loop(0, tokens // ROWS, split_own, 0)
+
+    def split_remote(index, carry):
+        kv_copy(index).wait_recv()
+        rows = pl.ds(pl.multiple_of(index * ROWS, ROWS), ROWS)
+        there = pl.ds(pl.multiple_of(tokens + index * ROWS, ROWS), ROWS)
+        for head in range(head_count):
+            low = head * HEAD_SIZE + kv_shift
+            key[head, there, :HEAD_SIZE] = remote_kv[rows, low : low + HEAD_SIZE]
+            low += attended
+            value[head, there, :HEAD_SIZE] = remote_kv[rows, low : low + HEAD_SIZE]
+        return carry
+
+    lax.fori_loop(0, tokens // ROWS, split_remote, 0)
+    loads[1].wait()
+
+    def forward_copy(source, target):
+        return pltpu.make_async_remote_copy(
+            src_ref=outgoing.at[target],
+            dst_ref=gathered.at[source],
+            send_sem=fwd_send.at[target],
+            recv_sem=fwd_recv.at[source],
+            device_id={"frame": target},
+            device_id_type=MESH,
+        )
+
+    def query_step(index, carry):
+        pair = lax.rem(my_pair + 1 + index, pairs)
+        rows = pl.ds(pl.multiple_of(pair * chunk, chunk), chunk)
+
+        def head_step(half, inner):
+            for part in range(2):
+                head = half * 2 + part
+                scores = lax.dot_general(
+                    query[head, rows, :],
+                    key[head],
+                    (((1,), (1,)), ((), ())),
+                    preferred_element_type=f32,
+                )
+                top = jnp.max(scores, axis=-1, keepdims=True)
+                weight = jnp.exp2(scores - top).astype(bf16)
+                total = jnp.dot(weight, value[head], preferred_element_type=f32)
+                head_out[head] = (total / total[:, HEAD_SIZE : HEAD_SIZE + 1]).astype(bf16)
+            return inner
+
+        lax.fori_loop(0, head_count // 2, head_step, 0)
+        for head in range(head_count):
+            mixed[:, head * HEAD_SIZE : (head + 1) * HEAD_SIZE] = head_out[head, :, :HEAD_SIZE]
+        product = jnp.dot(mixed[...], spatial_out[...], preferred_element_type=f32)
+        lines = hidden[rows, :].astype(f32) + gate * product
+        residual[rows, :] = lines
+        sent = (lines + placed[...]).astype(bf16)
+        for part in range(PAIR):
+            target = pair * PAIR + part
+            outgoing[target] = sent[part * item : (part + 1) * item]
+
+            @pl.when(target != me)
+            def _():
+                forward_copy(me, target).start()
+
+            @pl.when(target == me)
+            def _():
+                gathered[target] = sent[part * item : (part + 1) * item]
+
+        return carry
+
+    lax.fori_loop(0, pairs, query_step, 0)
+    loads[2].wait()
+
+    def temporal_step(index, carry):
+        pair = lax.rem(my_pair + 2 * pairs - 1 - index, pairs)
+        for part in range(PAIR):
+            source = pair * PAIR + part
+
+            @pl.when(source != me)
+            def _():
+                forward_copy(source, source).wait_recv()
+
+        lines = gathered[pl.ds(pair * PAIR, PAIR)].reshape(chunk, width)
+        product = jnp.dot(lines, temporal_qkv[...], preferred_element_type=f32)
+        temporal[pl.ds(pair * PAIR, PAIR)] = (
+            (product * column_factor).astype(bf16).reshape(PAIR, item, 3 * attended)
+        )
+        return carry
+
+    lax.fori_loop(0, pairs, temporal_step, 0)
+
+    count = peers * GROUP
+    row_item = lax.rem(lax.broadcasted_iota(jnp.int32, (count, count), 0), GROUP)
+    column_item = lax.rem(lax.broadcasted_iota(jnp.int32, (count, count), 1), GROUP)
+    same_item = row_item == column_item
+    lowest = float(jnp.finfo(f32).min)
+    half_item = item // 2
+
+    def return_copy(source, target, half):
+        rows = pl.ds(pl.multiple_of(half * half_item, half_item), half_item)
+        return pltpu.make_async_remote_copy(
+            src_ref=answer.at[target, rows, :],
+            dst_ref=returned.at[source, rows, :],
+            send_sem=ret_send.at[target, half],
+            recv_sem=ret_recv.at[source, half],
+            device_id={"frame": target},
+            device_id_type=MESH,
+        )
+
+    def half_step(half, carry):
+        def group_step(group, inner):
+            start = pl.multiple_of(half * half_item + group * GROUP, GROUP)
+            rows = pl.ds(start, GROUP)
+            lines = temporal[:, rows, :].reshape(count, 3 * attended)
+            for head in range(head_count):
+                low = head * HEAD_SIZE
+                scores = lax.dot_general(
+                    lines[:, low : low + HEAD_SIZE],
+                    lines[:, attended + low : attended + low + HEAD_SIZE],
+                    (((1,), (1,)), ((), ())),
+                    preferred_element_type=f32,
+                )
+                scores = jnp.where(same_item, scores, lowest)
+                top = jnp.max(scores, axis=-1, keepdims=True)
+                weight = jnp.exp2(scores - top).astype(bf16)
+                denominator = jnp.sum(weight.astype(f32), axis=-1, keepdims=True)
+                total = jnp.dot(
+                    weight,
+                    lines[:, 2 * attended + low : 2 * attended + low + HEAD_SIZE],
+                    preferred_element_type=f32,
+                )
+                answer[:, rows, low : low + HEAD_SIZE] = (
+                    (total / denominator).astype(bf16).reshape(peers, GROUP, HEAD_SIZE)
+                )
+            return inner
+
+        lax.fori_loop(0, half_item // GROUP, group_step, 0)
+
+        def send_step(step, inner):
+            return_copy(me, lax.rem(me + step, peers), half).start()
+            return inner
+
+        lax.fori_loop(1, peers, send_step, 0)
+        return carry
+
+    lax.fori_loop(0, 2, half_step, 0)
+    returned[me] = answer[me]
+    loads[3].wait()
+
+    velocity_rows = chunk * (width // width) // 8
+    lane = lax.broadcasted_iota(jnp.int32, (chunk, LANES), 1)
+    line = lax.broadcasted_iota(jnp.int32, (chunk, LANES), 0)
+    keep = lane // (LANES // 8) == lax.rem(line, 8)
+
+    def final_step(index, carry):
+        pair = lax.rem(my_pair + index, pairs)
+        for part in range(PAIR):
+            source = pair * PAIR + part
+
+            @pl.when(source != me)
+            def _():
+                return_copy(source, source, 0).wait_recv()
+                return_copy(source, source, 1).wait_recv()
+
+        rows = pl.ds(pl.multiple_of(pair * chunk, chunk), chunk)
+        lines = returned[pl.ds(pair * PAIR, PAIR)].reshape(chunk, attended)
+        product = jnp.dot(lines, temporal_out[...], preferred_element_type=f32)
+        block = residual[rows, :] + gate * product
+        hidden_out[rows, :] = block.astype(bf16)
+        final_rows = (layer_norm(block) * gain[...]).astype(bf16)
+        wide = jnp.dot(final_rows, wide_weight[...], preferred_element_type=f32)
+        packed = jnp.sum(jnp.where(keep, wide, 0.0).reshape(velocity_rows, 8, LANES), axis=1)
+        velocity_out[pl.ds(pl.multiple_of(pair * velocity_rows, velocity_rows), velocity_rows), :] = (
+            packed
+        )
+        return carry
+
+    lax.fori_loop(0, pairs, final_step, 0)
+    update_sent[...] = (latents[...] + time_delta[0, 0] * velocity_out[...]).astype(bf16)
+    next_copy = pltpu.make_async_remote_copy(
+        src_ref=update_sent,
+        dst_ref=update_received,
+        send_sem=next_send,
+        recv_sem=next_recv,
+        device_id={"frame": lax.rem(me + 1, peers)},
+        device_id_type=MESH,
+    )
+    next_copy.start()
+
+    def drain(index, carry):
+        kv_copy(index).wait_send()
+        return carry
+
+    lax.fori_loop(0, tokens // ROWS, drain, 0)
+
+    def drain_peer(step, carry):
+        target = lax.rem(me + step, peers)
+        forward_copy(me, target).wait_send()
+        return_copy(me, target, 0).wait_send()
+        return_copy(me, target, 1).wait_send()
+        return carry
+
+    lax.fori_loop(1, peers, drain_peer, 0)
+    next_copy.wait()
+
+    @pl.when(me == 0)
+    def _():
+        next_out[...] = noise[...]
+
+    @pl.when(me != 0)
+    def _():
+        next_out[...] = update_received[...].astype(f32)
+
+
+def body(
+    hidden_in,
+    latents,
+    fresh_noise,
+    level_index,
+    time_table,
+    frame_offset,
+    mod_table,
+    time_weight,
+    spatial_qkv,
+    spatial_out,
+    temporal_qkv,
+    temporal_out,
+    final_gain,
+    out_weight,
+):
+    tokens, width = hidden_in.shape[1:]
+    attended = spatial_out.shape[0]
+    head_count = attended // HEAD_SIZE
+    peers = lax.axis_size("frame")
+    item = tokens // peers
+    fits = (
+        peers % PAIR == 0
+        and tokens % ROWS == 0
+        and item % (2 * GROUP) == 0
+        and head_count % 2 == 0
+        and lax.axis_size("band") == 2
+        and peers * GROUP <= LANES
+        and out_weight.shape[1] * 8 == LANES
+    )
+    if not fits:
+        return plain_body(
+            hidden_in,
+            latents,
+            fresh_noise,
+            level_index,
+            time_table,
+            frame_offset,
+            mod_table,
+            time_weight,
+            spatial_qkv,
+            spatial_out,
+            temporal_qkv,
+            temporal_out,
+            final_gain,
+            out_weight,
+        )
+    table_index = jnp.arange(time_table.shape[0], dtype=jnp.int32)
+    now_steps = jnp.sum(
+        jnp.where(table_index[None, :] == level_index[:, None], time_table[None, :], 0), axis=1
+    )
+    next_steps = jnp.sum(
+        jnp.where(table_index[None, :] == level_index[:, None] - 1, time_table[None, :], 0), axis=1
+    )
+    activated = jax.nn.silu(sinusoid(now_steps, time_weight.shape[0], False)).astype(jnp.bfloat16)
+    modulation = mod_table[None, :] + jnp.dot(
+        activated, time_weight, preferred_element_type=jnp.float32
+    )
+    placed = sinusoid(lax.axis_index("frame") + frame_offset, width, True)
+    time_delta = ((next_steps - now_steps).astype(jnp.float32) / 1000.0).reshape(1, 1)
+    wide_weight = jnp.tile(out_weight, (1, 8))
+    bf16, f32 = jnp.bfloat16, jnp.float32
+    vmem = pl.BlockSpec(memory_space=pltpu.VMEM)
+    anywhere = pl.BlockSpec(memory_space=pl.ANY)
+    steps = tokens // ROWS
+    chunk = PAIR * item
+    dma = pltpu.SemaphoreType.DMA
+    latent_rows = latents.shape[1]
+    hidden_out, velocity, next_latents = pl.pallas_call(
+        functools.partial(block_kernel, peers, head_count),
+        out_shape=(
+            jax.ShapeDtypeStruct((tokens, width), bf16),
+            jax.ShapeDtypeStruct((latent_rows, LANES), f32),
+            jax.ShapeDtypeStruct((latent_rows, LANES), f32),
+        ),
+        in_specs=[vmem] * 5
+        + [pl.BlockSpec(memory_space=pltpu.SMEM)]
+        + [vmem] * 2
+        + [anywhere] * 4,
+        out_specs=(vmem, vmem, vmem),
+        scratch_shapes=[
+            pltpu.VMEM(spatial_qkv.shape, bf16),
+            pltpu.VMEM(spatial_out.shape, bf16),
+            pltpu.VMEM(temporal_qkv.shape, bf16),
+            pltpu.VMEM(temporal_out.shape, bf16),
+            pltpu.VMEM((tokens, width), bf16),
+            pltpu.VMEM((tokens, 3 * attended), bf16),
+            pltpu.VMEM((tokens, 3 * attended - attended // LANES * LANES), bf16),
+            pltpu.VMEM((head_count, tokens, LANES), bf16),
+            pltpu.VMEM((head_count, 2 * tokens, LANES), bf16),
+            pltpu.VMEM((head_count, 2 * tokens, LANES), bf16),
+            pltpu.VMEM((head_count, chunk, LANES), bf16),
+            pltpu.VMEM((chunk, attended), bf16),
+            pltpu.VMEM((tokens, width), f32),
+            pltpu.VMEM((peers, item, width), bf16),
+            pltpu.VMEM((peers, item, width), bf16),
+            pltpu.VMEM((peers, item, 3 * attended), bf16),
+            pltpu.VMEM((peers, item, attended), bf16),
+            pltpu.VMEM((peers, item, attended), bf16),
+            pltpu.VMEM((latent_rows, LANES), bf16),
+            pltpu.VMEM((latent_rows, LANES), bf16),
+            dma((4,)),
+            dma((steps,)),
+            dma((steps,)),
+            dma((peers,)),
+            dma((peers,)),
+            dma((peers, 2)),
+            dma((peers, 2)),
+            dma,
+            dma,
+        ],
+        compiler_params=pltpu.CompilerParams(
+            collective_id=0, has_side_effects=True, vmem_limit_bytes=63 * 1024 * 1024
+        ),
+        name="block",
+    )(
+        hidden_in[0],
+        modulation,
+        placed,
+        final_gain[None, :],
+        wide_weight,
+        time_delta,
+        latents[0],
+        fresh_noise,
+        spatial_qkv,
+        spatial_out,
+        temporal_qkv,
+        temporal_out,
+    )
+    return (hidden_out[None], velocity[None], next_latents[None])
+
+
 def solution(mesh):
     placed = (
         P(("groups", "frame"), "band", None),

time: 234 us -> 127 us (0.54)
  Pallas kernels: 0 us -> 98.9 us
  matrix products: 60.7 us -> 0.3 us
  blocking collectives: 47.3 us -> 0 us
  waiting for transfers between devices: 37.1 us -> 0 us
  other arithmetic: 24.2 us -> 2.84 us
  local copies, waits for them, and re-layouts: 38.9 us -> 20.6 us
  between operations: 17.7 us -> 3.84 us
  starting transfers between devices: 6.96 us -> 0 us
    pallas_call x0 -> x1, Pallas kernels: none -> 98.9 us  [body(): pl.pallas_call(functools.partial(block_kernel, peers, head_count), out_sh...]
    dot_general x9 -> x0, matrix products: 59.3 us -> none  [the longest x1 16.7 us: body(): jnp.einsum('leq,qlr->ler', attention_weight, value_matrix_rows, preferred...]
    all_to_all x1 -> x0, blocking collectives: 47.3 us -> none  [body(): lax.all_to_all(spread_rows, 'frame', split_axis=1, concat_axis=0, tiled=T...]
    all_to_all x1 -> x0, waiting for transfers between devices: 20.9 us -> none  [body(): lax.all_to_all(mixed_pairs, 'frame', split_axis=0, concat_axis=1, tiled=T...]
    reduce_sum x4 -> x0, other arithmetic: 20.9 us -> none  [the longest x1 16.7 us: body(): denominator = jnp.sum(attention_weight, axis=-1, dtype=jnp.float32)]
    all_gather x1 -> x0, waiting for transfers between devices: 14.7 us -> none  [body(): block_rows = lax.all_gather(key_value, 'band', axis=0, tiled=True)]
    slice x5 -> x0, local copies, waits for them, and re-layouts: 8.8 us -> none  [the longest x1 3.95 us: mix_frames(): parted[:, :, 2]]
    another operation x2, local copies, waits for them, and re-layouts: 9.49 us -> 1.68 us  [body(): wide_weight = jnp.tile(out_weight, (1, 8))]
  transfers between devices with their start and end apart: 3 -> 0, of which waited for: 3 -> 0; matrix products, arithmetic and copies ran while one was open for 0% -> 0% of each run, Pallas kernels for 0% -> 0%
where the time goes in v1:
time: 127 us; the launch traced here: 126 us
  Pallas kernels  98.9 us (78%)
  local copies, waits for them, and re-layouts  20.6 us (16%)
  between operations  3.84 us (3%)
  other arithmetic  2.84 us (2%)
    pallas_call x1, Pallas kernels, body(): pl.pallas_call(functools.partial(block_kernel, peers, head_count), out_sh...  98.9 us
    unnamed x11, local copies, waits for them, and re-layouts  17 us

profile of v1, /device:TPU:0, one launch (start us, length us, event | category | flops | bytes accessed | tf_op | source)
XLA Modules:
  0.0 126.5 jit_solution(9609680483099752893)
XLA Ops:
  0.6 0.0 copy-start
  2.0 1.3 %fusion.3 = (s32[]{:T(128)}, s32[]{:T(128)}) fusion(s32[32]{0:T(128)} %param.18, s32[]{:T(128)} %bitcast.6, s32[]{:T(128)} %bitcast.15), kind=kLoop, calls=%fused_computation.9 | loop fusion | flops 190 | bytes 144 | tf_op jit(solution)/shard_map/reduce_sum | solution.py:551
  5.1 1.3 %broadcast_in_dim.14.gain = f32[1,1152]{1,0:T(1,128)} reshape(f32[1152]{0:T(1024)} %param.26) | data formatting | bytes 9216 | tf_op jit(solution)/shard_map/broadcast_in_dim | solution.py:619
  6.4 0.1 fusion
  6.5 0.7 pad_maximum_fusion.placed
  7.2 0.0 copy-done
  7.2 0.3 convolution_reduce_fusion
  7.5 0.7 add.21
  8.3 0.6 add.22.mod
  8.9 0.8 tile.4
  9.7 0.9 copy.20.wide_weight
  10.5 6.4 %copy.21.spatial_qkv_hbm = bf16[1152,1728]{1,0:T(8,128)(2,1)} copy(bf16[1152,1728]{0,1:T(8,128)(2,1)} %param.22) | data formatting | bytes 7962624 | tf_op args[8]
  17.0 6.5 %copy.22.temporal_qkv_hbm = bf16[1152,1728]{1,0:T(8,128)(2,1)} copy(bf16[1152,1728]{0,1:T(8,128)(2,1)} %param.24) | data formatting | bytes 7962624 | tf_op args[10]
  23.5 98.9 %block.1 = (bf16[768,1152]{1,0:T(8,128)(2,1)}, f32[96,128]{1,0:T(8,128)}, f32[96,128]{1,0:T(8,128)}) custom-call(bf16[768,1152]{1,0:T(8,128)(2,1)} %bitcast.17, f32[1,3456]{1,0:T(1,128)} %add.22.mod, f32[1,1152]{1,0:T(1,128)} %pad_maximum_fusion.placed, f32[1,1152]{1,0:T(1,128)} %broadcast_in_dim.14.gain, bf16[1152,128]{1,0:T(8,128)(2,1)} %copy.20.wide_weight, ...), custom_call_target="tpu_custom_call" | custom-call | tf_op jit(solution)/shard_map/block/pallas_call | solution.py:568
  122.4 0.0 copy-start.2
  122.4 0.0 copy-start.1
  122.4 2.8 %copy.28 = bf16[1,768,1152]{2,1,0:T(8,128)(2,1)} copy(bf16[1,768,1152]{2,1,0:T(8,128)(2,1)} %bitcast.16) | data formatting | bytes 3538944
  125.2 0.0 copy-done.2
  125.2 0.6 copy.29
  125.9 0.0 copy-done.1
  125.9 0.6 copy.30
  (1 shorter events, 0.0 us)
Async XLA Ops:
  0.6 6.6 %copy-start = (bf16[128,3456]{1,0:T(8,128)(2,1)S(1)}, bf16[128,3456]{1,0:T(8,128)(2,1)}, u32[]{:S(2)}) copy-start(bf16[128,3456]{1,0:T(8,128)(2,1)} %param.21) | copy-start | bytes 2654212
  122.4 2.9 %copy-start.2 = (f32[96,128]{1,0:T(8,128)S(1)}, f32[96,128]{1,0:T(8,128)}, u32[]{:S(2)}) copy-start(f32[96,128]{1,0:T(8,128)} %get-tuple-element.7) | copy-start | bytes 147460
  122.4 3.5 %copy-start.1 = (f32[96,128]{1,0:T(8,128)S(1)}, f32[96,128]{1,0:T(8,128)}, u32[]{:S(2)}) copy-start(f32[96,128]{1,0:T(8,128)} %get-tuple-element.8) | copy-start | bytes 147460

commit v2 on v1

--- a/solution.py
+++ b/solution.py
@@ -3,6 +3,7 @@
 
 import jax
 import jax.numpy as jnp
+import numpy as np
 from jax import lax
 from jax.experimental import pallas as pl
 from jax.experimental.pallas import tpu as pltpu
@@ -157,15 +158,25 @@
 LANES = 128
 
 
+def times_turned(rows, turned):
+    return lax.dot_general(
+        rows, turned, (((1,), (1,)), ((), ())), preferred_element_type=jnp.float32
+    )
+
+
 def block_kernel(
     peers,
     head_count,
     hidden,
-    mod,
-    placed,
-    gain,
-    wide_weight,
-    time_delta,
+    level_index,
+    time_table,
+    frame_offset,
+    time_frequency,
+    place_frequency,
+    mod_table,
+    time_weight,
+    final_gain,
+    out_weight,
     latents,
     noise,
     spatial_qkv_hbm,
@@ -187,6 +198,10 @@
     value,
     head_out,
     mixed,
+    mod,
+    placed,
+    gain,
+    wide_weight,
     residual,
     outgoing,
     gathered,
@@ -239,6 +254,22 @@
             barrier, inc=1, device_id={"frame": lax.rem(me + step, peers)}, device_id_type=MESH
         )
 
+    table = time_table[...].reshape(1, time_table.shape[0]).astype(f32)
+    entry = lax.broadcasted_iota(jnp.int32, table.shape, 1)
+    level = level_index[0]
+    now_step = jnp.sum(jnp.where(entry == level, table, 0.0), axis=1, keepdims=True)
+    next_step = jnp.sum(jnp.where(entry == level - 1, table, 0.0), axis=1, keepdims=True)
+    time_delta = (next_step - now_step) / 1000.0
+    angles = now_step * time_frequency[...]
+    activated = jax.nn.silu(jnp.concatenate([jnp.cos(angles), jnp.sin(angles)], axis=-1))
+    mod[...] = mod_table[...].reshape(1, 3 * width) + jnp.dot(
+        activated.astype(bf16), time_weight[...], preferred_element_type=f32
+    )
+    places = (me + frame_offset[0]).astype(f32) * place_frequency[...]
+    placed[...] = jnp.concatenate([jnp.sin(places), jnp.cos(places)], axis=-1)
+    gain[...] = final_gain[...].reshape(1, width)
+    for copy in range(8):
+        wide_weight[copy * (LANES // 8) : (copy + 1) * (LANES // 8), :] = out_weight[...]
     column = lax.broadcasted_iota(jnp.int32, (1, 3 * attended), 1)
     column_factor = jnp.where(column < attended, query_factor, 1.0).astype(f32)
     gate = mod[:, 2 * width :]
@@ -269,7 +300,7 @@
 
     def project_step(index, carry):
         rows = pl.ds(pl.multiple_of(index * ROWS, ROWS), ROWS)
-        product = jnp.dot(normed[rows, :], spatial_qkv[...], preferred_element_type=f32)
+        product = times_turned(normed[rows, :], spatial_qkv[...])
         projected[rows, :] = (product * column_factor).astype(bf16)
         kv_copy(index).start()
         return carry
@@ -366,7 +397,7 @@
                 forward_copy(source, source).wait_recv()
 
         lines = gathered[pl.ds(pair * PAIR, PAIR)].reshape(chunk, width)
-        product = jnp.dot(lines, temporal_qkv[...], preferred_element_type=f32)
+        product = times_turned(lines, temporal_qkv[...])
         temporal[pl.ds(pair * PAIR, PAIR)] = (
             (product * column_factor).astype(bf16).reshape(PAIR, item, 3 * attended)
         )
@@ -432,7 +463,7 @@
     returned[me] = answer[me]
     loads[3].wait()
 
-    velocity_rows = chunk * (width // width) // 8
+    velocity_rows = chunk // 8
     lane = lax.broadcasted_iota(jnp.int32, (chunk, LANES), 1)
     line = lax.broadcasted_iota(jnp.int32, (chunk, LANES), 0)
     keep = lane // (LANES // 8) == lax.rem(line, 8)
@@ -453,7 +484,7 @@
         block = residual[rows, :] + gate * product
         hidden_out[rows, :] = block.astype(bf16)
         final_rows = (layer_norm(block) * gain[...]).astype(bf16)
-        wide = jnp.dot(final_rows, wide_weight[...], preferred_element_type=f32)
+        wide = times_turned(final_rows, wide_weight[...])
         packed = jnp.sum(jnp.where(keep, wide, 0.0).reshape(velocity_rows, 8, LANES), axis=1)
         velocity_out[pl.ds(pl.multiple_of(pair * velocity_rows, velocity_rows), velocity_rows), :] = (
             packed
@@ -461,7 +492,7 @@
         return carry
 
     lax.fori_loop(0, pairs, final_step, 0)
-    update_sent[...] = (latents[...] + time_delta[0, 0] * velocity_out[...]).astype(bf16)
+    update_sent[...] = (latents[...] + time_delta * velocity_out[...]).astype(bf16)
     next_copy = pltpu.make_async_remote_copy(
         src_ref=update_sent,
         dst_ref=update_received,
@@ -544,20 +575,10 @@
             final_gain,
             out_weight,
         )
-    table_index = jnp.arange(time_table.shape[0], dtype=jnp.int32)
-    now_steps = jnp.sum(
-        jnp.where(table_index[None, :] == level_index[:, None], time_table[None, :], 0), axis=1
-    )
-    next_steps = jnp.sum(
-        jnp.where(table_index[None, :] == level_index[:, None] - 1, time_table[None, :], 0), axis=1
-    )
-    activated = jax.nn.silu(sinusoid(now_steps, time_weight.shape[0], False)).astype(jnp.bfloat16)
-    modulation = mod_table[None, :] + jnp.dot(
-        activated, time_weight, preferred_element_type=jnp.float32
-    )
-    placed = sinusoid(lax.axis_index("frame") + frame_offset, width, True)
-    time_delta = ((next_steps - now_steps).astype(jnp.float32) / 1000.0).reshape(1, 1)
-    wide_weight = jnp.tile(out_weight, (1, 8))
+    def frequency(half):
+        steps = np.arange(half, dtype=np.float64)
+        return np.exp(-math.log(10000.0) * steps / half).astype(np.float32)[None, :]
+
     bf16, f32 = jnp.bfloat16, jnp.float32
     vmem = pl.BlockSpec(memory_space=pltpu.VMEM)
     anywhere = pl.BlockSpec(memory_space=pl.ANY)
@@ -572,15 +593,15 @@
             jax.ShapeDtypeStruct((latent_rows, LANES), f32),
             jax.ShapeDtypeStruct((latent_rows, LANES), f32),
         ),
-        in_specs=[vmem] * 5
-        + [pl.BlockSpec(memory_space=pltpu.SMEM)]
-        + [vmem] * 2
+        in_specs=[vmem]
+        + [pl.BlockSpec(memory_space=pltpu.SMEM), vmem, pl.BlockSpec(memory_space=pltpu.SMEM)]
+        + [vmem] * 8
         + [anywhere] * 4,
         out_specs=(vmem, vmem, vmem),
         scratch_shapes=[
-            pltpu.VMEM(spatial_qkv.shape, bf16),
+            pltpu.VMEM(spatial_qkv.shape[::-1], bf16),
             pltpu.VMEM(spatial_out.shape, bf16),
-            pltpu.VMEM(temporal_qkv.shape, bf16),
+            pltpu.VMEM(temporal_qkv.shape[::-1], bf16),
             pltpu.VMEM(temporal_out.shape, bf16),
             pltpu.VMEM((tokens, width), bf16),
             pltpu.VMEM((tokens, 3 * attended), bf16),
@@ -590,6 +611,10 @@
             pltpu.VMEM((head_count, 2 * tokens, LANES), bf16),
             pltpu.VMEM((head_count, chunk, LANES), bf16),
             pltpu.VMEM((chunk, attended), bf16),
+            pltpu.VMEM((1, 3 * width), f32),
+            pltpu.VMEM((1, width), f32),
+            pltpu.VMEM((1, width), f32),
+            pltpu.VMEM((LANES, width), bf16),
             pltpu.VMEM((tokens, width), f32),
             pltpu.VMEM((peers, item, width), bf16),
             pltpu.VMEM((peers, item, width), bf16),
@@ -614,16 +639,20 @@
         name="block",
     )(
         hidden_in[0],
-        modulation,
-        placed,
-        final_gain[None, :],
-        wide_weight,
-        time_delta,
+        level_index,
+        time_table,
+        frame_offset,
+        frequency(time_weight.shape[0] // 2),
+        frequency(width // 2),
+        mod_table,
+        time_weight,
+        final_gain,
+        out_weight.T,
         latents[0],
         fresh_noise,
-        spatial_qkv,
+        spatial_qkv.T,
         spatial_out,
-        temporal_qkv,
+        temporal_qkv.T,
         temporal_out,
     )
     return (hidden_out[None], velocity[None], next_latents[None])

time: 127 us -> 107 us (0.84)
  local copies, waits for them, and re-layouts: 20.6 us -> 4.09 us
  other arithmetic: 2.84 us -> 0 us
  Pallas kernels: 98.9 us -> 101 us
  between operations: 3.84 us -> 1.95 us
    unnamed x11 -> x7, local copies, waits for them, and re-layouts: 17 us -> 4.09 us
    pallas_call x1, Pallas kernels: 98.9 us -> 101 us  [body(): pl.pallas_call(functools.partial(block_kernel, peers, head_count), out_sh...]
    another operation x2 -> x0, local copies, waits for them, and re-layouts: 1.68 us -> none  [body(): wide_weight = jnp.tile(out_weight, (1, 8))]
    broadcast_in_dim x1 -> x0, local copies, waits for them, and re-layouts: 1.3 us -> none  [body(): final_gain[None, :]]
    reduce_sum x1 -> x0, other arithmetic: 1.29 us -> none  [body(): jnp.sum(jnp.where(table_index[None, :] == level_index[:, None] - 1, time_...]
where the time goes in v2:
time: 107 us
  Pallas kernels  101 us (94%)
  local copies, waits for them, and re-layouts  4.09 us (4%)
  between operations  1.95 us (2%)
    pallas_call x1, Pallas kernels, body(): pl.pallas_call(functools.partial(block_kernel, peers, head_count), out_sh...  101 us
    unnamed x7, local copies, waits for them, and re-layouts  4.09 us

profile of v2, /device:TPU:0, one launch (start us, length us, event | category | flops | bytes accessed | tf_op | source)
XLA Modules:
  0.0 106.8 jit_solution(4950759622767956789)
XLA Ops:
  1.9 100.8 %block.1 = (bf16[768,1152]{1,0:T(8,128)(2,1)}, f32[96,128]{1,0:T(8,128)}, f32[96,128]{1,0:T(8,128)}) custom-call(bf16[768,1152]{1,0:T(8,128)(2,1)} %bitcast.11, s32[1]{0:T(128)S(6)} %copy.22.level_index, s32[32]{0:T(128)} %time_table.1, s32[1]{0:T(128)S(6)} %copy.23.frame_offset, f32[1,64]{1,0:T(1,128)} %constant.4.clone.time_frequency, ...), custom_call_target="tpu_custom_call" | custom-call | tf_op jit(solution)/shard_map/block/pallas_call | solution.py:589
  102.7 0.0 copy-start.1
  102.7 0.0 copy-start
  102.7 2.8 %copy.24 = bf16[1,768,1152]{2,1,0:T(8,128)(2,1)} copy(bf16[1,768,1152]{2,1,0:T(8,128)(2,1)} %bitcast.10) | data formatting | bytes 3538944
  105.6 0.0 copy-done.1
  105.6 0.6 copy.25
  106.2 0.0 copy-done
  106.2 0.6 copy.26
Async XLA Ops:
  102.7 2.9 %copy-start.1 = (f32[96,128]{1,0:T(8,128)S(1)}, f32[96,128]{1,0:T(8,128)}, u32[]{:S(2)}) copy-start(f32[96,128]{1,0:T(8,128)} %get-tuple-element.7) | copy-start | bytes 147460
  102.7 3.5 %copy-start = (f32[96,128]{1,0:T(8,128)S(1)}, f32[96,128]{1,0:T(8,128)}, u32[]{:S(2)}) copy-start(f32[96,128]{1,0:T(8,128)} %get-tuple-element.8) | copy-start | bytes 147460

commit v3 on v2

--- a/solution.py
+++ b/solution.py
@@ -210,6 +210,13 @@
     returned,
     update_sent,
     update_received,
+    far_hidden,
+    far_mixed,
+    far_gate,
+    gate_sent,
+    mixed_sent,
+    early_send,
+    early_recv,
     weight_sem,
     kv_send,
     kv_recv,
@@ -265,8 +272,17 @@
     mod[...] = mod_table[...].reshape(1, 3 * width) + jnp.dot(
         activated.astype(bf16), time_weight[...], preferred_element_type=f32
     )
-    places = (me + frame_offset[0]).astype(f32) * place_frequency[...]
-    placed[...] = jnp.concatenate([jnp.sin(places), jnp.cos(places)], axis=-1)
+    gate_sent[...] = mod[:, 2 * width :]
+
+    def placement(frame):
+        places = (frame + frame_offset[0]).astype(f32) * place_frequency[...]
+        return jnp.concatenate([jnp.sin(places), jnp.cos(places)], axis=-1)
+
+    placed[0:1, :] = placement(me)
+    for part in range(PAIR):
+        placed[part + 1 : part + 2, :] = placement(
+            lax.rem(my_pair + pairs // 2, pairs) * PAIR + part
+        )
     gain[...] = final_gain[...].reshape(1, width)
     for copy in range(8):
         wide_weight[copy * (LANES // 8) : (copy + 1) * (LANES // 8), :] = out_weight[...]
@@ -281,10 +297,52 @@
         return carry
 
     lax.fori_loop(0, tokens // 64, norm_step, 0)
-    query[...] = jnp.zeros_like(query)
-    key[...] = jnp.zeros_like(key)
-    value[...] = jnp.ones_like(value)
+    for heads in (query, key):
+        heads[:, :, HEAD_SIZE:] = jnp.zeros(heads.shape[:2] + (LANES - HEAD_SIZE,), bf16)
+    value[:, :, HEAD_SIZE:] = jnp.ones(value.shape[:2] + (LANES - HEAD_SIZE,), bf16)
     pl.semaphore_wait(barrier, peers)
+    far_pair = lax.rem(my_pair + pairs // 2, pairs)
+    my_part = lax.rem(me, PAIR)
+
+    def early_copies(part):
+        target = far_pair * PAIR + part
+        rows = pl.ds(pl.multiple_of(target * item, item), item)
+        return [
+            pltpu.make_async_remote_copy(
+                src_ref=source,
+                dst_ref=place,
+                send_sem=early_send.at[part, kind],
+                recv_sem=early_recv.at[my_part, kind],
+                device_id={"frame": target},
+                device_id_type=MESH,
+            )
+            for kind, (source, place) in enumerate(
+                (
+                    (gate_sent, far_gate.at[my_part]),
+                    (hidden.at[rows, :], far_hidden.at[my_part]),
+                    (mixed_sent.at[part], far_mixed.at[my_part]),
+                )
+            )
+        ]
+
+    def early_arrivals(part):
+        return [
+            pltpu.make_async_remote_copy(
+                src_ref=place,
+                dst_ref=place,
+                send_sem=early_send.at[part, kind],
+                recv_sem=early_recv.at[part, kind],
+                device_id={"frame": far_pair * PAIR + part},
+                device_id_type=MESH,
+            )
+            for kind, place in enumerate(
+                (far_gate.at[part], far_hidden.at[part], far_mixed.at[part])
+            )
+        ]
+
+    for part in range(PAIR):
+        early_copies(part)[0].start()
+        early_copies(part)[1].start()
     loads[0].wait()
 
     def kv_copy(index):
@@ -369,18 +427,32 @@
         product = jnp.dot(mixed[...], spatial_out[...], preferred_element_type=f32)
         lines = hidden[rows, :].astype(f32) + gate * product
         residual[rows, :] = lines
-        sent = (lines + placed[...]).astype(bf16)
-        for part in range(PAIR):
-            target = pair * PAIR + part
-            outgoing[target] = sent[part * item : (part + 1) * item]
-
-            @pl.when(target != me)
-            def _():
-                forward_copy(me, target).start()
-
-            @pl.when(target == me)
-            def _():
-                gathered[target] = sent[part * item : (part + 1) * item]
+        sent = (lines + placed[0:1, :]).astype(bf16)
+
+        @pl.when(pair == far_pair)
+        def _():
+            for part in range(PAIR):
+                mixed_sent[part] = mixed[part * item : (part + 1) * item, :]
+                early_copies(part)[2].start()
+
+        @pl.when(pair != far_pair)
+        def _():
+            for part in range(PAIR):
+                outgoing[pair * PAIR + part] = sent[part * item : (part + 1) * item]
+            for part in range(PAIR):
+                target = pair * PAIR + part
+
+                @pl.when(target != me)
+                def _():
+                    forward_copy(me, target).start()
+
+        @pl.when(pair == my_pair)
+        def _():
+            for part in range(PAIR):
+
+                @pl.when(my_part == part)
+                def _():
+                    gathered[me] = sent[part * item : (part + 1) * item]
 
         return carry
 
@@ -389,12 +461,30 @@
 
     def temporal_step(index, carry):
         pair = lax.rem(my_pair + 2 * pairs - 1 - index, pairs)
-        for part in range(PAIR):
-            source = pair * PAIR + part
-
-            @pl.when(source != me)
-            def _():
-                forward_copy(source, source).wait_recv()
+        @pl.when(pair == far_pair)
+        def _():
+            for part in range(PAIR):
+                for copy in early_arrivals(part):
+                    copy.wait_recv()
+            product = jnp.dot(
+                far_mixed[...].reshape(chunk, attended), spatial_out[...], preferred_element_type=f32
+            )
+            for part in range(PAIR):
+                lines = far_hidden[part].astype(f32) + (
+                    far_gate[part] * product[part * item : (part + 1) * item]
+                )
+                gathered[far_pair * PAIR + part] = (
+                    lines + placed[part + 1 : part + 2, :]
+                ).astype(bf16)
+
+        @pl.when(pair != far_pair)
+        def _():
+            for part in range(PAIR):
+                source = pair * PAIR + part
+
+                @pl.when(source != me)
+                def _():
+                    forward_copy(source, source).wait_recv()
 
         lines = gathered[pl.ds(pair * PAIR, PAIR)].reshape(chunk, width)
         product = times_turned(lines, temporal_qkv[...])
@@ -410,56 +500,52 @@
     column_item = lax.rem(lax.broadcasted_iota(jnp.int32, (count, count), 1), GROUP)
     same_item = row_item == column_item
     lowest = float(jnp.finfo(f32).min)
-    half_item = item // 2
-
-    def return_copy(source, target, half):
-        rows = pl.ds(pl.multiple_of(half * half_item, half_item), half_item)
+    groups = item // GROUP
+    ones = jnp.ones((count, HEAD_SIZE), bf16)
+
+    def return_copy(source, target, group):
+        rows = pl.ds(pl.multiple_of(group * GROUP, GROUP), GROUP)
         return pltpu.make_async_remote_copy(
             src_ref=answer.at[target, rows, :],
             dst_ref=returned.at[source, rows, :],
-            send_sem=ret_send.at[target, half],
-            recv_sem=ret_recv.at[source, half],
+            send_sem=ret_send.at[target, group],
+            recv_sem=ret_recv.at[source, group],
             device_id={"frame": target},
             device_id_type=MESH,
         )
 
-    def half_step(half, carry):
-        def group_step(group, inner):
-            start = pl.multiple_of(half * half_item + group * GROUP, GROUP)
-            rows = pl.ds(start, GROUP)
-            lines = temporal[:, rows, :].reshape(count, 3 * attended)
-            for head in range(head_count):
-                low = head * HEAD_SIZE
-                scores = lax.dot_general(
-                    lines[:, low : low + HEAD_SIZE],
-                    lines[:, attended + low : attended + low + HEAD_SIZE],
-                    (((1,), (1,)), ((), ())),
-                    preferred_element_type=f32,
-                )
-                scores = jnp.where(same_item, scores, lowest)
-                top = jnp.max(scores, axis=-1, keepdims=True)
-                weight = jnp.exp2(scores - top).astype(bf16)
-                denominator = jnp.sum(weight.astype(f32), axis=-1, keepdims=True)
-                total = jnp.dot(
-                    weight,
-                    lines[:, 2 * attended + low : 2 * attended + low + HEAD_SIZE],
-                    preferred_element_type=f32,
-                )
-                answer[:, rows, low : low + HEAD_SIZE] = (
-                    (total / denominator).astype(bf16).reshape(peers, GROUP, HEAD_SIZE)
-                )
+    def group_step(group, carry):
+        rows = pl.ds(pl.multiple_of(group * GROUP, GROUP), GROUP)
+        lines = temporal[:, rows, :].reshape(count, 3 * attended)
+        for head in range(head_count):
+            low = head * HEAD_SIZE
+            scores = lax.dot_general(
+                lines[:, low : low + HEAD_SIZE],
+                lines[:, attended + low : attended + low + HEAD_SIZE],
+                (((1,), (1,)), ((), ())),
+                preferred_element_type=f32,
+            )
+            scores = jnp.where(same_item, scores, lowest)
+            top = jnp.max(scores, axis=-1, keepdims=True)
+            weight = jnp.exp2(scores - top).astype(bf16)
+            denominator = jnp.dot(weight, ones, preferred_element_type=f32)
+            total = jnp.dot(
+                weight,
+                lines[:, 2 * attended + low : 2 * attended + low + HEAD_SIZE],
+                preferred_element_type=f32,
+            )
+            answer[:, rows, low : low + HEAD_SIZE] = (
+                (total / denominator).astype(bf16).reshape(peers, GROUP, HEAD_SIZE)
+            )
+
+        def send_step(step, inner):
+            return_copy(me, lax.rem(me + step, peers), group).start()
             return inner
 
-        lax.fori_loop(0, half_item // GROUP, group_step, 0)
-
-        def send_step(step, inner):
-            return_copy(me, lax.rem(me + step, peers), half).start()
-            return inner
-
         lax.fori_loop(1, peers, send_step, 0)
         return carry
 
-    lax.fori_loop(0, 2, half_step, 0)
+    lax.fori_loop(0, groups, group_step, 0)
     returned[me] = answer[me]
     loads[3].wait()
 
@@ -475,8 +561,8 @@
 
             @pl.when(source != me)
             def _():
-                return_copy(source, source, 0).wait_recv()
-                return_copy(source, source, 1).wait_recv()
+                for group in range(groups):
+                    return_copy(source, source, group).wait_recv()
 
         rows = pl.ds(pl.multiple_of(pair * chunk, chunk), chunk)
         lines = returned[pl.ds(pair * PAIR, PAIR)].reshape(chunk, attended)
@@ -511,12 +597,19 @@
 
     def drain_peer(step, carry):
         target = lax.rem(me + step, peers)
-        forward_copy(me, target).wait_send()
-        return_copy(me, target, 0).wait_send()
-        return_copy(me, target, 1).wait_send()
+
+        @pl.when(target // PAIR != far_pair)
+        def _():
+            forward_copy(me, target).wait_send()
+
+        for group in range(groups):
+            return_copy(me, target, group).wait_send()
         return carry
 
     lax.fori_loop(1, peers, drain_peer, 0)
+    for part in range(PAIR):
+        for copy in early_copies(part):
+            copy.wait_send()
     next_copy.wait()
 
     @pl.when(me == 0)
@@ -550,7 +643,7 @@
     peers = lax.axis_size("frame")
     item = tokens // peers
     fits = (
-        peers % PAIR == 0
+        peers % (2 * PAIR) == 0
         and tokens % ROWS == 0
         and item % (2 * GROUP) == 0
         and head_count % 2 == 0
@@ -612,7 +705,7 @@
             pltpu.VMEM((head_count, chunk, LANES), bf16),
             pltpu.VMEM((chunk, attended), bf16),
             pltpu.VMEM((1, 3 * width), f32),
-            pltpu.VMEM((1, width), f32),
+            pltpu.VMEM((8, width), f32),
             pltpu.VMEM((1, width), f32),
             pltpu.VMEM((LANES, width), bf16),
             pltpu.VMEM((tokens, width), f32),
@@ -623,13 +716,20 @@
             pltpu.VMEM((peers, item, attended), bf16),
             pltpu.VMEM((latent_rows, LANES), bf16),
             pltpu.VMEM((latent_rows, LANES), bf16),
+            pltpu.VMEM((PAIR, item, width), bf16),
+            pltpu.VMEM((PAIR, item, attended), bf16),
+            pltpu.VMEM((PAIR, 1, width), f32),
+            pltpu.VMEM((1, width), f32),
+            pltpu.VMEM((PAIR, item, attended), bf16),
+            dma((PAIR, 3)),
+            dma((PAIR, 3)),
             dma((4,)),
             dma((steps,)),
             dma((steps,)),
             dma((peers,)),
             dma((peers,)),
-            dma((peers, 2)),
-            dma((peers, 2)),
+            dma((peers, item // GROUP)),
+            dma((peers, item // GROUP)),
             dma,
             dma,
         ],

time: 107 us -> 102 us (0.953); the launches traced: 107 us -> 100 us
  Pallas kernels: 101 us -> 94.2 us
    pallas_call x1, Pallas kernels: 101 us -> 94.2 us  [body(): pl.pallas_call(functools.partial(block_kernel, peers, head_count), out_sh...]
where the time goes in v3:
time: 102 us; the launch traced here: 100 us
  Pallas kernels  94.2 us (92%)
  local copies, waits for them, and re-layouts  4.09 us (4%)
  between operations  1.95 us (2%)
    pallas_call x1, Pallas kernels, body(): pl.pallas_call(functools.partial(block_kernel, peers, head_count), out_sh...  94.2 us
    unnamed x7, local copies, waits for them, and re-layouts  4.09 us

profile of v3, /device:TPU:0, one launch (start us, length us, event | category | flops | bytes accessed | tf_op | source)
XLA Modules:
  0.0 100.3 jit_solution(6966320013315295657)
XLA Ops:
  1.9 94.2 %block.1 = (bf16[768,1152]{1,0:T(8,128)(2,1)}, f32[96,128]{1,0:T(8,128)}, f32[96,128]{1,0:T(8,128)}) custom-call(bf16[768,1152]{1,0:T(8,128)(2,1)} %bitcast.11, s32[1]{0:T(128)S(6)} %copy.22.level_index, s32[32]{0:T(128)} %time_table.1, s32[1]{0:T(128)S(6)} %copy.23.frame_offset, f32[1,64]{1,0:T(1,128)} %constant.4.clone.time_frequency, ...), custom_call_target="tpu_custom_call" | custom-call | tf_op jit(solution)/shard_map/block/pallas_call | solution.py:682
  96.1 0.0 copy-start.1
  96.2 0.0 copy-start
  96.2 2.8 %copy.24 = bf16[1,768,1152]{2,1,0:T(8,128)(2,1)} copy(bf16[1,768,1152]{2,1,0:T(8,128)(2,1)} %bitcast.10) | data formatting | bytes 3538944
  99.0 0.0 copy-done.1
  99.0 0.6 copy.25
  99.6 0.0 copy-done
  99.6 0.6 copy.26
Async XLA Ops:
  96.1 2.9 %copy-start.1 = (f32[96,128]{1,0:T(8,128)S(1)}, f32[96,128]{1,0:T(8,128)}, u32[]{:S(2)}) copy-start(f32[96,128]{1,0:T(8,128)} %get-tuple-element.7) | copy-start | bytes 147460
  96.2 3.5 %copy-start = (f32[96,128]{1,0:T(8,128)S(1)}, f32[96,128]{1,0:T(8,128)}, u32[]{:S(2)}) copy-start(f32[96,128]{1,0:T(8,128)} %get-tuple-element.8) | copy-start | bytes 147460
